TPU v7x, 512 devices: a whole 4x8x8 slice. The times are simulated.
512 devices in a mesh: lang: 64 (over y, z), rep: 8 (over x, core).
Axes of the slice: x: 4, y: 8, z: 8, core: 2. Of those that a mesh axis runs over, the one named last changes fastest.
Arguments:
- tokens: bfloat16 [65536, 1024], P(('lang', 'rep')), may hold values from -24 to 24
- grad_out: bfloat16 [65536, 1024], P(('lang', 'rep')), may hold values from -24 to 24
- lang_ids: int32 [65536], P(('lang', 'rep')), may hold values from 0 to 7, as said below
- slot_ids: int32 [65536], P(('lang', 'rep')), may hold values from 0 to 23, as said below
- w_up: bfloat16 [1024, 32768], P(None, 'lang'), may hold values from -0.1875 to 0.1875
- w_down_t: bfloat16 [1024, 32768], P(None, 'lang'), may hold values from -0.09375 to 0.09375
Outputs:
- ffn_out: bfloat16 [65536, 1024], P(('lang', 'rep'))
- grad_tokens: bfloat16 [65536, 1024], P(('lang', 'rep'))
- grad_up: float32 [1024, 32768], P('rep', 'lang')
- grad_down: float32 [1024, 32768], P('rep', 'lang')
Inputs may be any that keep to these rules, and one draw needn't show every extreme that they name: `lang_ids`: each device holds 128 consecutive tokens. On every device one language, the same on all devices, has exactly 24 tokens; every other language has at most 18 tokens on a device, and on every device one of them has exactly 18. `slot_ids`: on each device the tokens of one language hold the distinct slots 0 to their count minus 1, in no particular order.
All inputs are finite; a program needn't handle non-finite values.
Results may differ from a plain program's by a relative error of at most 0.0058.
Values may be sent and summed in bfloat16 or wider, within the bound.
A program may use at most 128 MiB of HBM per device.

v0:
```python
import jax
import jax.numpy as jnp
from jax import lax
from jax.sharding import Mesh
from jax.sharding import PartitionSpec as P

MODULES = 8
TOK_DEV = 128
CAPACITY = 18
INV_ROOT_TWO = 0.7071067811865476
INV_ROOT_TAU = 0.3989422804014327


def gelu_value(values):
    return 0.5 * values * (1.0 + lax.erf(values * INV_ROOT_TWO))


def gelu_slope(values):
    return (
        0.5 * (1.0 + lax.erf(values * INV_ROOT_TWO))
        + values * jnp.exp(-0.5 * values * values) * INV_ROOT_TAU
    )


def per_device(tokens, grad_out, lang_ids, slot_ids, w_up, w_down_t):
    feature_width = tokens.shape[1]
    capacity = CAPACITY
    keep_mask = slot_ids < capacity
    target = jnp.where(keep_mask, lang_ids * capacity + slot_ids, MODULES * capacity)
    safe_slot = jnp.minimum(slot_ids, capacity - 1)
    token_scale = 1.0 / TOK_DEV

    def place(values):
        buffer = (
            jnp.zeros((MODULES * capacity, feature_width), values.dtype)
            .at[target]
            .set(values, mode="drop")
        )
        return buffer.reshape(MODULES, capacity, feature_width)

    def dispatch(values):
        by_y = lax.all_to_all(place(values), "ly", split_axis=0, concat_axis=0, tiled=True)
        every = lax.all_gather(by_y, "lz", axis=0, tiled=True)
        return every.reshape(-1, feature_width)

    def give_back(rows):
        parts = rows.astype(jnp.float32).reshape(-1, capacity, feature_width)
        summed = lax.psum_scatter(parts, "lz", scatter_dimension=0, tiled=True)
        summed = summed.astype(jnp.bfloat16)
        return lax.all_to_all(summed, "ly", split_axis=0, concat_axis=0, tiled=True)

    def collect(returned):
        picked = returned[lang_ids, safe_slot]
        return jnp.where(keep_mask[:, None], picked, jnp.zeros_like(picked))

    flat_tokens = dispatch(tokens)
    flat_grads = dispatch(grad_out)
    pre_flat = jnp.dot(flat_tokens, w_up, preferred_element_type=jnp.float32)
    hidden_flat = gelu_value(pre_flat).astype(jnp.bfloat16)
    partial_rows = lax.dot_general(
        hidden_flat, w_down_t, (((1,), (1,)), ((), ())), preferred_element_type=jnp.float32
    ).astype(jnp.bfloat16)
    returned = give_back(partial_rows)
    grad_down = lax.psum_scatter(
        lax.dot_general(
            flat_grads, hidden_flat, (((0,), (0,)), ((), ())), preferred_element_type=jnp.float32
        )
        * token_scale,
        "rep",
        scatter_dimension=0,
        tiled=True,
    )
    d_hidden = jnp.dot(flat_grads, w_down_t, preferred_element_type=jnp.float32)
    d_pre = (d_hidden * gelu_slope(pre_flat)).astype(jnp.bfloat16)
    grad_up = lax.psum_scatter(
        lax.dot_general(
            flat_tokens, d_pre, (((0,), (0,)), ((), ())), preferred_element_type=jnp.float32
        )
        * token_scale,
        "rep",
        scatter_dimension=0,
        tiled=True,
    )
    dx_part = lax.dot_general(
        d_pre, w_up, (((1,), (1,)), ((), ())), preferred_element_type=jnp.float32
    ).astype(jnp.bfloat16)
    dx_back = give_back(dx_part)
    return (collect(returned), collect(dx_back), grad_up, grad_down)


def solution(mesh):
    n_lang = mesh.shape["lang"]
    groups = n_lang // MODULES
    devices = mesh.devices.reshape(MODULES, groups, mesh.shape["rep"])
    split_mesh = Mesh(devices, ("ly", "lz", "rep"))
    rows = P(("ly", "lz", "rep"), None)
    ids = P(("ly", "lz", "rep"))
    cols = P(None, ("ly", "lz"))
    return jax.shard_map(
        per_device,
        mesh=split_mesh,
        in_specs=(rows, rows, ids, ids, cols, cols),
        out_specs=(rows, rows, P("rep", ("ly", "lz")), P("rep", ("ly", "lz"))),
        check_vma=False,
    )
```

profile of v0, /device:TPU:8, one launch (start us, length us, event | category | flops | bytes accessed | tf_op | source)
XLA Modules:
  0.0 392.5 jit_solution(12223299433012391685)
XLA Ops:
  7.2 0.0 copy-start
  7.2 0.0 all-gather.5.cloned.1.call-start
  7.2 0.8 fusion.13
  8.0 1.6 scatter_custom_fusion.1
  9.6 0.1 reshape.37
  9.7 20.6 %all_to_all.20 = bf16[8,18,1024]{2,1,0:T(8,128)(2,1)S(1)} all-to-all(bf16[8,18,1024]{2,1,0:T(8,128)(2,1)S(1)} %reshape.37), channel_id=1, replica_groups=mesh['ly'=8,'lz'=8,'rep'=8] {'ly'}, dimensions={0} | all-to-all | bytes 589824 | tf_op jit(solution)/shard_map/all_to_all | solution.py:42
  30.3 0.9 copy.17
  31.2 0.0 all-gather.5.cloned.1.call-update
  31.2 0.0 all-gather.3.cloned.1.call-start
  31.2 1.6 scatter_custom_fusion
  32.9 0.1 reshape.33
  33.0 15.6 %all_to_all.21 = bf16[8,18,1024]{2,1,0:T(8,128)(2,1)S(1)} all-to-all(bf16[8,18,1024]{2,1,0:T(8,128)(2,1)S(1)} %reshape.33), channel_id=1, replica_groups=mesh['ly'=8,'lz'=8,'rep'=8] {'ly'}, dimensions={0} | all-to-all | bytes 589824 | tf_op jit(solution)/shard_map/all_to_all | solution.py:42
  48.6 0.9 copy.14
  49.5 0.0 all-gather.3.cloned.1.call-update
  49.5 0.0 reduce-scatter.7.cloned.1.call-start
  49.6 27.2 %all-gather.5.cloned.1.call-done = bf16[64,18,1024]{2,0,1:T(8,128)(2,1)} async-done(((bf16[8,18,1024]{2,0,1:T(8,128)(2,1)}), bf16[64,18,1024]{2,0,1:T(8,128)(2,1)}) %all-gather.5.cloned.1.call-update) | async-done | bytes 2359312 | tf_op jit(solution)/shard_map/all_gather | solution.py:43
  76.8 4.7 %copy.18 = bf16[64,18,1024]{2,1,0:T(8,128)(2,1)} copy(bf16[64,18,1024]{2,0,1:T(8,128)(2,1)} %all-gather.5.cloned.1.call-done) | data formatting | bytes 4718592 | tf_op jit(solution)/shard_map/all_gather | solution.py:43
  81.5 2.9 reshape.38
  84.4 37.9 %all-gather.3.cloned.1.call-done = bf16[64,18,1024]{2,0,1:T(8,128)(2,1)} async-done(((bf16[8,18,1024]{2,0,1:T(8,128)(2,1)}), bf16[64,18,1024]{2,0,1:T(8,128)(2,1)}) %all-gather.3.cloned.1.call-update) | async-done | bytes 2359312 | tf_op jit(solution)/shard_map/all_gather | solution.py:43
  122.3 4.7 %copy.15 = bf16[64,18,1024]{2,1,0:T(8,128)(2,1)} copy(bf16[64,18,1024]{2,0,1:T(8,128)(2,1)} %all-gather.3.cloned.1.call-done) | data formatting | bytes 4718592 | tf_op jit(solution)/shard_map/all_gather | solution.py:43
  127.0 4.3 %reshape.34 = bf16[1152,1024]{1,0:T(8,128)(2,1)} reshape(bf16[64,18,1024]{2,1,0:T(8,128)(2,1)} %copy.15) | data formatting | bytes 4718592 | tf_op jit(solution)/shard_map/reshape | solution.py:44
  131.4 0.0 copy-done
  131.4 0.0 copy-start.2
  131.4 4.4 %multiply_convert_fusion = (bf16[1152,512]{1,0:T(8,128)(2,1)}, f32[1152,512]{1,0:T(8,128)S(1)}) fusion(bf16[1152,1024]{1,0:T(8,128)(2,1)} %reshape.34, bf16[1024,512]{1,0:T(8,128)(2,1)S(1)} %copy-done), kind=kOutput, calls=%fused_computation.15 | convolution fusion | flops 1210908672 | bytes 6946816 | tf_op jit(solution)/shard_map/dot_general | solution.py:58
  135.7 0.0 copy-done.2
  135.7 2.0 fusion.2
  137.8 0.0 copy-start.3
  137.8 1.0 copy-done.3
  138.8 3.7 fusion.1
  142.4 5.6 %reshape.44 = f32[64,18,1024]{2,1,0:T(8,128)} reshape(f32[1152,1024]{1,0:T(8,128)} %fusion.1) | data formatting | bytes 9437184 | tf_op jit(solution)/shard_map/reshape | solution.py:47
  148.0 0.0 reduce-scatter.7.cloned.1.call-update
  148.1 0.0 reduce-scatter.5.cloned.1.call-start
  148.1 5.1 %fusion = f32[1152,1024]{1,0:T(8,128)} fusion(bf16[1152,512]{1,0:T(8,128)(2,1)} %get-tuple-element.8, bf16[1024,512]{1,0:T(8,128)(2,1)} %param.11), kind=kOutput, calls=%fused_computation.6 | convolution fusion | flops 1210318848 | bytes 6946816 | tf_op jit(solution)/shard_map/dot_general | solution.py:60
  153.2 5.6 %reshape.42 = f32[64,18,1024]{2,1,0:T(8,128)} reshape(f32[1152,1024]{1,0:T(8,128)} %fusion) | data formatting | bytes 9437184 | tf_op jit(solution)/shard_map/reshape | solution.py:47
  158.8 0.0 reduce-scatter.5.cloned.1.call-update
  158.8 0.0 reduce-scatter.9.cloned.1.call-start
  158.8 5.2 %convolution_multiply_fusion.2 = f32[1024,512]{1,0:T(8,128)} fusion(bf16[1152,1024]{1,0:T(8,128)(2,1)} %reshape.34, bf16[1152,512]{1,0:T(8,128)(2,1)} %copy-done.3), kind=kOutput, calls=%fused_computation.18 | convolution fusion | flops 1208483840 | bytes 5636096 | tf_op jit(solution)/shard_map/dot_general | solution.py:76
  164.1 0.0 reduce-scatter.9.cloned.1.call-update
  164.1 0.2 reduce-scatter.11.cloned.1.call-start
  164.3 4.1 %convolution_multiply_fusion.1 = f32[1024,512]{1,0:T(8,128)} fusion(bf16[1152,1024]{1,0:T(8,128)(2,1)S(1)} %reshape.38, bf16[1152,512]{1,0:T(8,128)(2,1)} %get-tuple-element.8), kind=kOutput, calls=%fused_computation.17 | convolution fusion | flops 1208483840 | bytes 5636096 | tf_op jit(solution)/shard_map/dot_general | solution.py:65
  168.5 0.0 reduce-scatter.11.cloned.1.call-update
  168.5 0.0 copy-start.1
  168.5 56.3 %reduce-scatter.7.cloned.1.call-done = f32[8,18,1024]{2,1,0:T(8,128)} async-done(((f32[64,18,1024]{2,1,0:T(8,128)}), f32[8,18,1024]{2,1,0:T(8,128)}) %reduce-scatter.7.cloned.1.call-update) | async-done | bytes 589840 | tf_op jit(solution)/shard_map/reduce_scatter | solution.py:48
  224.8 1.9 convert_element_type.25
  226.7 7.3 %all-to-all-start.3 = ((bf16[8,18,1024]{2,1,0:T(8,128)(2,1)}), bf16[8,18,1024]{2,1,0:T(8,128)(2,1)S(1)}, u32[]{:S(2)}, u32[]{:S(2)}) async-start(bf16[8,18,1024]{2,1,0:T(8,128)(2,1)} %convert_element_type.25), calls=%async_computation.5 | async-start | bytes 786432 | tf_op jit(solution)/shard_map/all_to_all | solution.py:50
  234.0 70.2 %reduce-scatter.5.cloned.1.call-done = f32[8,18,1024]{2,1,0:T(8,128)} async-done(((f32[64,18,1024]{2,1,0:T(8,128)}), f32[8,18,1024]{2,1,0:T(8,128)}) %reduce-scatter.5.cloned.1.call-update) | async-done | bytes 589840 | tf_op jit(solution)/shard_map/reduce_scatter | solution.py:48
  304.2 1.9 convert_element_type.22
  306.1 0.0 all-to-all-done.3
  306.1 7.3 %all-to-all-start.1 = ((bf16[8,18,1024]{2,1,0:T(8,128)(2,1)}), bf16[8,18,1024]{2,1,0:T(8,128)(2,1)S(1)}, u32[]{:S(2)}, u32[]{:S(2)}) async-start(bf16[8,18,1024]{2,1,0:T(8,128)(2,1)} %convert_element_type.22), calls=%async_computation.2 | async-start | bytes 786432 | tf_op jit(solution)/shard_map/all_to_all | solution.py:50
  313.4 0.0 copy-done.1
  313.4 0.2 copy.19
  313.6 1.6 gather_fusion.1
  315.2 11.5 %all-to-all-done.1 = bf16[8,18,1024]{2,1,0:T(8,128)(2,1)S(1)} async-done(((bf16[8,18,1024]{2,1,0:T(8,128)(2,1)}), bf16[8,18,1024]{2,1,0:T(8,128)(2,1)S(1)}, u32[]{:S(2)}, u32[]{:S(2)}) %all-to-all-start.1) | async-done | bytes 294944 | tf_op jit(solution)/shard_map/all_to_all | solution.py:50
  326.7 0.2 copy.16
  326.9 1.6 gather_fusion
  328.5 0.9 broadcast_select_fusion
  329.4 15.3 %reduce-scatter.9.cloned.1.call-done = f32[128,512]{1,0:T(8,128)} async-done(((f32[1024,512]{1,0:T(8,128)}), f32[128,512]{1,0:T(8,128)}) %reduce-scatter.9.cloned.1.call-update) | async-done | bytes 262160 | tf_op jit(solution)/shard_map/reduce_scatter | solution.py:75
  344.6 41.0 %reduce-scatter.11.cloned.1.call-done = f32[128,512]{1,0:T(8,128)} async-done(((f32[1024,512]{1,0:T(8,128)}), f32[128,512]{1,0:T(8,128)}) %reduce-scatter.11.cloned.1.call-update) | async-done | bytes 262160 | tf_op jit(solution)/shard_map/reduce_scatter | solution.py:64
  (1 shorter events, 0.0 us)
Async XLA Ops:
  7.2 124.2 %copy-start = (bf16[1024,512]{1,0:T(8,128)(2,1)S(1)}, bf16[1024,512]{1,0:T(8,128)(2,1)}, u32[]{:S(2)}) copy-start(bf16[1024,512]{1,0:T(8,128)(2,1)} %param.10) | copy-start | bytes 3145732
  7.2 69.6 %all-gather.5.cloned.1.call-start = ((), (), s32[]{:S(2)}) async-start(), calls=%async_computation.10 | async-start | bytes 2654208 | tf_op jit(solution)/shard_map/all_gather | solution.py:43
  31.2 91.1 %all-gather.3.cloned.1.call-start = ((), (), s32[]{:S(2)}) async-start(), calls=%async_computation.8 | async-start | bytes 2654208 | tf_op jit(solution)/shard_map/all_gather | solution.py:43
  49.5 175.3 %reduce-scatter.7.cloned.1.call-start = ((), (), s32[]{:S(2)}) async-start(), calls=%async_computation.11 | async-start | bytes 7077888 | tf_op jit(solution)/shard_map/reduce_scatter | solution.py:48
  131.4 4.4 %copy-start.2 = (bf16[1024,512]{1,0:T(8,128)(2,1)S(1)}, bf16[1024,512]{1,0:T(8,128)(2,1)}, u32[]{:S(2)}) copy-start(bf16[1024,512]{1,0:T(8,128)(2,1)} %param.11) | copy-start | bytes 3145732
  137.8 1.0 copy-start.3
  148.1 156.1 %reduce-scatter.5.cloned.1.call-start = ((), (), s32[]{:S(2)}) async-start(), calls=%async_computation.9 | async-start | bytes 7077888 | tf_op jit(solution)/shard_map/reduce_scatter | solution.py:48
  158.8 185.8 %reduce-scatter.9.cloned.1.call-start = ((), (), s32[]{:S(2)}) async-start(), calls=%async_computation.12 | async-start | bytes 2359296 | tf_op jit(solution)/shard_map/reduce_scatter | solution.py:75
  164.1 221.5 %reduce-scatter.11.cloned.1.call-start = ((), (), s32[]{:S(2)}) async-start(), calls=%async_computation.13 | async-start | bytes 2359296 | tf_op jit(solution)/shard_map/reduce_scatter | solution.py:64
  168.5 144.9 %copy-start.1 = (s32[128]{0:T(128)S(1)}, s32[128]{0:T(128)}, u32[]{:S(2)}) copy-start(s32[128]{0:T(128)} %param.9) | copy-start | bytes 1540
  226.7 79.4 %all-to-all-start.3 = ((bf16[8,18,1024]{2,1,0:T(8,128)(2,1)}), bf16[8,18,1024]{2,1,0:T(8,128)(2,1)S(1)}, u32[]{:S(2)}, u32[]{:S(2)}) async-start(bf16[8,18,1024]{2,1,0:T(8,128)(2,1)} %convert_element_type.25), calls=%async_computation.5 | async-start | bytes 786432 | tf_op jit(solution)/shard_map/all_to_all | solution.py:50
  306.1 20.6 %all-to-all-start.1 = ((bf16[8,18,1024]{2,1,0:T(8,128)(2,1)}), bf16[8,18,1024]{2,1,0:T(8,128)(2,1)S(1)}, u32[]{:S(2)}, u32[]{:S(2)}) async-start(bf16[8,18,1024]{2,1,0:T(8,128)(2,1)} %convert_element_type.22), calls=%async_computation.2 | async-start | bytes 786432 | tf_op jit(solution)/shard_map/all_to_all | solution.py:50
Sparse Core Ops, SparseCore 0:
  31.3 45.4 all-gather.4
  78.9 43.4 all-gather.2
  148.2 76.5 reduce-scatter.6
  227.5 76.6 reduce-scatter.4
  307.4 37.1 reduce-scatter.8
  347.9 37.6 reduce-scatter.10
where the time goes:
time: 393 us; the launch traced here: 392 us
  waiting for transfers between devices  259 us (66%)
  local copies, waits for them, and re-layouts  37.6 us (10%)
  blocking collectives  36.2 us (9%)
  matrix products  24.5 us (6%)
  starting transfers between devices  15 us (4%)
  between operations  14.2 us (4%)
  other arithmetic  5.53 us (1%)
    reduce_scatter x2, waiting for transfers between devices, give_back(): summed = lax.psum_scatter(parts, 'lz', scatter_dimension=0, tiled=True)  126 us
    all_gather x2, waiting for transfers between devices, dispatch(): every = lax.all_gather(by_y, 'lz', axis=0, tiled=True)  65.2 us
    reduce_scatter x1, waiting for transfers between devices, per_device(): lax.psum_scatter(lax.dot_general(flat_grads, hidden_flat, (((0,), (0,)),...  41 us
    all_to_all x2, blocking collectives, dispatch(): lax.all_to_all(place(values), 'ly', split_axis=0, concat_axis=0, tiled=True)  36.2 us
    reduce_scatter x1, waiting for transfers between devices, per_device(): lax.psum_scatter(lax.dot_general(flat_tokens, d_pre, (((0,), (0,)), ((),...  15.3 us
    all_to_all x2, starting transfers between devices, give_back(): return lax.all_to_all(summed, 'ly', split_axis=0, concat_axis=0, tiled=True)  14.6 us
    all_to_all x2, waiting for transfers between devices, give_back(): return lax.all_to_all(summed, 'ly', split_axis=0, concat_axis=0, tiled=True)  11.5 us
    reshape x2, local copies, waits for them, and re-layouts, give_back(): parts = rows.astype(jnp.float32).reshape(-1, capacity, feature_width)  11.2 us
  transfers between devices with their start and end apart: 8, of which 7 were waited for; matrix products, arithmetic and copies ran while one was open for 10% of the time, Pallas kernels for 0%

commit v1 on v0

--- a/solution.py
+++ b/solution.py
@@ -40,7 +40,8 @@
 
     def dispatch(values):
         by_y = lax.all_to_all(place(values), "ly", split_axis=0, concat_axis=0, tiled=True)
-        every = lax.all_gather(by_y, "lz", axis=0, tiled=True)
+        newest = jnp.stack(lax.axis_size("lz") * [by_y])
+        every = jnp.concatenate(lax.all_to_all(newest, "lz", 0, 0), axis=0)
         return every.reshape(-1, feature_width)
 
     def give_back(rows):

time: 393 us -> 447 us (1.14)
  waiting for transfers between devices: 259 us -> 313 us
  blocking collectives: 36.2 us -> 0 us
  starting transfers between devices: 15 us -> 46.3 us
  local copies, waits for them, and re-layouts: 37.6 us -> 42.4 us
    all_to_all x0 -> x4, waiting for transfers between devices: none -> 117 us  [the longest x2 98.5 us: dispatch(): every = jnp.concatenate(lax.all_to_all(newest, 'lz', 0, 0), axis=0)]
    all_gather x2 -> x0, waiting for transfers between devices: 65.2 us -> none  [dispatch(): every = lax.all_gather(by_y, 'lz', axis=0, tiled=True)]
    all_to_all x2 -> x0, blocking collectives: 36.2 us -> none  [dispatch(): lax.all_to_all(place(values), 'ly', split_axis=0, concat_axis=0, tiled=True)]
    all_to_all x0 -> x4, starting transfers between devices: none -> 31.5 us  [the longest x2 17.5 us: dispatch(): every = jnp.concatenate(lax.all_to_all(newest, 'lz', 0, 0), axis=0)]
    another operation x0 -> x4, local copies, waits for them, and re-layouts: none -> 11.6 us  [the longest x2 7.26 us: dispatch(): return every.reshape(-1, feature_width)]
    all_gather x2 -> x0, local copies, waits for them, and re-layouts: 9.35 us -> none  [dispatch(): every = lax.all_gather(by_y, 'lz', axis=0, tiled=True)]
    all_to_all x0 -> x2, local copies, waits for them, and re-layouts: none -> 8.01 us  [dispatch(): every = jnp.concatenate(lax.all_to_all(newest, 'lz', 0, 0), axis=0)]
    reshape x2 -> x0, local copies, waits for them, and re-layouts: 7.28 us -> none  [dispatch(): return every.reshape(-1, feature_width)]
  transfers between devices with their start and end apart: 8 -> 10, of which waited for: 7 -> 9; matrix products, arithmetic and copies ran while one was open for 10% -> 9% of each run, Pallas kernels for 0% -> 0%
where the time goes in v1:
time: 447 us; the launch traced here: 445 us
  waiting for transfers between devices  313 us (70%)
  starting transfers between devices  46.3 us (10%)
  local copies, waits for them, and re-layouts  42.4 us (9%)
  matrix products  24.2 us (5%)
  between operations  13.9 us (3%)
  other arithmetic  5.57 us (1%)
    reduce_scatter x2, waiting for transfers between devices, give_back(): summed = lax.psum_scatter(parts, 'lz', scatter_dimension=0, tiled=True)  127 us
    all_to_all x2, waiting for transfers between devices, dispatch(): every = jnp.concatenate(lax.all_to_all(newest, 'lz', 0, 0), axis=0)  98.5 us
    reduce_scatter x1, waiting for transfers between devices, per_device(): lax.psum_scatter(lax.dot_general(flat_grads, hidden_flat, (((0,), (0,)),...  40.9 us
    all_to_all x2, waiting for transfers between devices, dispatch(): lax.all_to_all(place(values), 'ly', split_axis=0, concat_axis=0, tiled=True)  18.9 us
    all_to_all x2, starting transfers between devices, dispatch(): every = jnp.concatenate(lax.all_to_all(newest, 'lz', 0, 0), axis=0)  17.5 us
    reduce_scatter x1, waiting for transfers between devices, per_device(): lax.psum_scatter(lax.dot_general(flat_tokens, d_pre, (((0,), (0,)), ((),...  15.5 us
    all_to_all x2, starting transfers between devices, give_back(): return lax.all_to_all(summed, 'ly', split_axis=0, concat_axis=0, tiled=True)  14.5 us
    all_to_all x2, starting transfers between devices, dispatch(): lax.all_to_all(place(values), 'ly', split_axis=0, concat_axis=0, tiled=True)  14 us
  transfers between devices with their start and end apart: 10, of which 9 were waited for; matrix products, arithmetic and copies ran while one was open for 9% of the time, Pallas kernels for 0%

profile of v1, /device:TPU:8, one launch (start us, length us, event | category | flops | bytes accessed | tf_op | source)
XLA Modules:
  0.0 445.3 jit_solution(15348253458804898525)
XLA Ops:
  7.2 0.0 copy-start
  7.2 0.8 fusion.13
  7.9 1.6 scatter_custom_fusion.1
  9.6 0.8 reshape.34
  10.4 9.2 %all-to-all-start.3 = ((bf16[8,18,1024]{2,1,0:T(8,128)(2,1)}), bf16[8,18,1024]{2,1,0:T(8,128)(2,1)S(1)}, u32[]{:S(2)}, u32[]{:S(2)}) async-start(bf16[8,18,1024]{2,1,0:T(8,128)(2,1)} %reshape.34), calls=%async_computation.4 | async-start | bytes 786432 | tf_op jit(solution)/shard_map/all_to_all | solution.py:42
  19.6 1.6 scatter_custom_fusion
  21.2 0.8 reshape.31
  22.1 9.1 %all-to-all-done.3 = bf16[8,18,1024]{2,1,0:T(8,128)(2,1)S(1)} async-done(((bf16[8,18,1024]{2,1,0:T(8,128)(2,1)}), bf16[8,18,1024]{2,1,0:T(8,128)(2,1)S(1)}, u32[]{:S(2)}, u32[]{:S(2)}) %all-to-all-start.3) | async-done | bytes 294944 | tf_op jit(solution)/shard_map/all_to_all | solution.py:42
  31.2 4.8 %all-to-all-start = ((bf16[8,18,1024]{2,1,0:T(8,128)(2,1)}), bf16[8,18,1024]{2,1,0:T(8,128)(2,1)S(1)}, u32[]{:S(2)}, u32[]{:S(2)}) async-start(bf16[8,18,1024]{2,1,0:T(8,128)(2,1)} %reshape.31), calls=%async_computation | async-start | bytes 786432 | tf_op jit(solution)/shard_map/all_to_all | solution.py:42
  36.0 0.2 copy.17
  36.2 9.8 %all-to-all-done = bf16[8,18,1024]{2,1,0:T(8,128)(2,1)S(1)} async-done(((bf16[8,18,1024]{2,1,0:T(8,128)(2,1)}), bf16[8,18,1024]{2,1,0:T(8,128)(2,1)S(1)}, u32[]{:S(2)}, u32[]{:S(2)}) %all-to-all-start) | async-done | bytes 294944 | tf_op jit(solution)/shard_map/all_to_all | solution.py:42
  46.0 0.0 copy-start.1
  46.0 1.7 stack.5
  47.8 0.0 copy-done.1
  47.8 13.1 %all-to-all-start.4 = ((bf16[8,8,18,1024]{3,1,2,0:T(8,128)(2,1)}), bf16[8,8,18,1024]{3,1,2,0:T(8,128)(2,1)S(1)}, u32[]{:S(2)}, u32[]{:S(2)}) async-start(bf16[8,8,18,1024]{3,1,2,0:T(8,128)(2,1)} %stack.5), calls=%async_computation.5 | async-start | bytes 4718592 | tf_op jit(solution)/shard_map/all_to_all | solution.py:44
  60.9 1.9 copy.14
  62.7 51.5 %all-to-all-done.4 = bf16[8,8,18,1024]{3,1,2,0:T(8,128)(2,1)S(1)} async-done(((bf16[8,8,18,1024]{3,1,2,0:T(8,128)(2,1)}), bf16[8,8,18,1024]{3,1,2,0:T(8,128)(2,1)S(1)}, u32[]{:S(2)}, u32[]{:S(2)}) %all-to-all-start.4) | async-done | bytes 2359328 | tf_op jit(solution)/shard_map/all_to_all | solution.py:44
  114.2 2.6 stack.4
  116.8 4.4 all-to-all-start.1
  121.2 0.0 reduce-scatter.7.cloned.1.call-start
  121.3 3.2 copy.18
  124.5 2.9 reshape_reshape.7
  127.4 47.1 %all-to-all-done.1 = bf16[8,8,18,1024]{3,1,2,0:T(8,128)(2,1)} async-done(((bf16[8,8,18,1024]{3,1,2,0:T(8,128)(2,1)}), bf16[8,8,18,1024]{3,1,2,0:T(8,128)(2,1)}, u32[]{:S(2)}, u32[]{:S(2)}) %all-to-all-start.1) | async-done | bytes 2359328 | tf_op jit(solution)/shard_map/all_to_all | solution.py:44
  174.4 4.8 %copy.15 = bf16[8,8,18,1024]{3,2,1,0:T(8,128)(2,1)} copy(bf16[8,8,18,1024]{3,1,2,0:T(8,128)(2,1)} %all-to-all-done.1) | data formatting | bytes 4718592 | tf_op jit(solution)/shard_map/all_to_all | solution.py:44
  179.3 4.3 reshape_reshape.6
  183.6 0.0 copy-done
  183.6 0.0 copy-start.3
  183.6 4.4 multiply_convert_fusion
  188.0 0.0 copy-done.3
  188.0 2.0 fusion.2
  190.0 0.0 copy-start.4
  190.0 1.0 copy-done.4
  191.1 3.6 fusion.1
  194.7 5.6 %reshape.40 = f32[64,18,1024]{2,1,0:T(8,128)} reshape(f32[1152,1024]{1,0:T(8,128)} %fusion.1) | data formatting | bytes 9437184 | tf_op jit(solution)/shard_map/reshape | solution.py:48
  200.3 0.0 reduce-scatter.7.cloned.1.call-update
  200.3 0.0 reduce-scatter.5.cloned.1.call-start
  200.4 5.1 %fusion = f32[1152,1024]{1,0:T(8,128)} fusion(bf16[1152,512]{1,0:T(8,128)(2,1)} %get-tuple-element.8, bf16[1024,512]{1,0:T(8,128)(2,1)} %param.11), kind=kOutput, calls=%fused_computation.6 | convolution fusion | flops 1210318848 | bytes 6946816 | tf_op jit(solution)/shard_map/dot_general | solution.py:61
  205.5 5.6 %reshape.38 = f32[64,18,1024]{2,1,0:T(8,128)} reshape(f32[1152,1024]{1,0:T(8,128)} %fusion) | data formatting | bytes 9437184 | tf_op jit(solution)/shard_map/reshape | solution.py:48
  211.1 0.0 reduce-scatter.5.cloned.1.call-update
  211.1 0.2 reduce-scatter.9.cloned.1.call-start
  211.3 4.9 %convolution_multiply_fusion.2 = f32[1024,512]{1,0:T(8,128)} fusion(bf16[1152,1024]{1,0:T(8,128)(2,1)} %reshape_reshape.6, bf16[1152,512]{1,0:T(8,128)(2,1)} %copy-done.4), kind=kOutput, calls=%fused_computation.18 | convolution fusion | flops 1208483840 | bytes 5636096 | tf_op jit(solution)/shard_map/dot_general | solution.py:77
  216.2 0.0 reduce-scatter.9.cloned.1.call-update
  216.3 0.0 reduce-scatter.11.cloned.1.call-start
  216.3 4.1 convolution_multiply_fusion.1
  220.5 0.0 reduce-scatter.11.cloned.1.call-update
  220.5 0.0 copy-start.2
  220.5 57.2 %reduce-scatter.7.cloned.1.call-done = f32[8,18,1024]{2,1,0:T(8,128)} async-done(((f32[64,18,1024]{2,1,0:T(8,128)}), f32[8,18,1024]{2,1,0:T(8,128)}) %reduce-scatter.7.cloned.1.call-update) | async-done | bytes 589840 | tf_op jit(solution)/shard_map/reduce_scatter | solution.py:49
  277.7 2.0 convert_element_type.25
  279.6 7.3 %all-to-all-start.5 = ((bf16[8,18,1024]{2,1,0:T(8,128)(2,1)}), bf16[8,18,1024]{2,1,0:T(8,128)(2,1)S(1)}, u32[]{:S(2)}, u32[]{:S(2)}) async-start(bf16[8,18,1024]{2,1,0:T(8,128)(2,1)} %convert_element_type.25), calls=%async_computation.7 | async-start | bytes 786432 | tf_op jit(solution)/shard_map/all_to_all | solution.py:51
  286.9 70.3 %reduce-scatter.5.cloned.1.call-done = f32[8,18,1024]{2,1,0:T(8,128)} async-done(((f32[64,18,1024]{2,1,0:T(8,128)}), f32[8,18,1024]{2,1,0:T(8,128)}) %reduce-scatter.5.cloned.1.call-update) | async-done | bytes 589840 | tf_op jit(solution)/shard_map/reduce_scatter | solution.py:49
  357.2 1.9 convert_element_type.22
  359.1 0.0 all-to-all-done.5
  359.1 7.3 %all-to-all-start.2 = ((bf16[8,18,1024]{2,1,0:T(8,128)(2,1)}), bf16[8,18,1024]{2,1,0:T(8,128)(2,1)S(1)}, u32[]{:S(2)}, u32[]{:S(2)}) async-start(bf16[8,18,1024]{2,1,0:T(8,128)(2,1)} %convert_element_type.22), calls=%async_computation.3 | async-start | bytes 786432 | tf_op jit(solution)/shard_map/all_to_all | solution.py:51
  366.4 0.0 copy-done.2
  366.4 0.2 copy.19
  366.6 1.6 gather_fusion.1
  368.2 11.5 %all-to-all-done.2 = bf16[8,18,1024]{2,1,0:T(8,128)(2,1)S(1)} async-done(((bf16[8,18,1024]{2,1,0:T(8,128)(2,1)}), bf16[8,18,1024]{2,1,0:T(8,128)(2,1)S(1)}, u32[]{:S(2)}, u32[]{:S(2)}) %all-to-all-start.2) | async-done | bytes 294944 | tf_op jit(solution)/shard_map/all_to_all | solution.py:51
  379.7 0.2 copy.16
  379.9 1.6 gather_fusion
  381.5 0.9 broadcast_select_fusion
  382.4 15.5 %reduce-scatter.9.cloned.1.call-done = f32[128,512]{1,0:T(8,128)} async-done(((f32[1024,512]{1,0:T(8,128)}), f32[128,512]{1,0:T(8,128)}) %reduce-scatter.9.cloned.1.call-update) | async-done | bytes 262160 | tf_op jit(solution)/shard_map/reduce_scatter | solution.py:76
  397.9 40.9 %reduce-scatter.11.cloned.1.call-done = f32[128,512]{1,0:T(8,128)} async-done(((f32[1024,512]{1,0:T(8,128)}), f32[128,512]{1,0:T(8,128)}) %reduce-scatter.11.cloned.1.call-update) | async-done | bytes 262160 | tf_op jit(solution)/shard_map/reduce_scatter | solution.py:65
  (1 shorter events, 0.0 us)
Async XLA Ops:
  7.2 176.5 %copy-start = (bf16[1024,512]{1,0:T(8,128)(2,1)S(1)}, bf16[1024,512]{1,0:T(8,128)(2,1)}, u32[]{:S(2)}) copy-start(bf16[1024,512]{1,0:T(8,128)(2,1)} %param.10) | copy-start | bytes 3145732
  10.4 20.8 %all-to-all-start.3 = ((bf16[8,18,1024]{2,1,0:T(8,128)(2,1)}), bf16[8,18,1024]{2,1,0:T(8,128)(2,1)S(1)}, u32[]{:S(2)}, u32[]{:S(2)}) async-start(bf16[8,18,1024]{2,1,0:T(8,128)(2,1)} %reshape.34), calls=%async_computation.4 | async-start | bytes 786432 | tf_op jit(solution)/shard_map/all_to_all | solution.py:42
  31.2 14.8 %all-to-all-start = ((bf16[8,18,1024]{2,1,0:T(8,128)(2,1)}), bf16[8,18,1024]{2,1,0:T(8,128)(2,1)S(1)}, u32[]{:S(2)}, u32[]{:S(2)}) async-start(bf16[8,18,1024]{2,1,0:T(8,128)(2,1)} %reshape.31), calls=%async_computation | async-start | bytes 786432 | tf_op jit(solution)/shard_map/all_to_all | solution.py:42
  46.0 1.7 copy-start.1
  47.8 66.4 %all-to-all-start.4 = ((bf16[8,8,18,1024]{3,1,2,0:T(8,128)(2,1)}), bf16[8,8,18,1024]{3,1,2,0:T(8,128)(2,1)S(1)}, u32[]{:S(2)}, u32[]{:S(2)}) async-start(bf16[8,8,18,1024]{3,1,2,0:T(8,128)(2,1)} %stack.5), calls=%async_computation.5 | async-start | bytes 4718592 | tf_op jit(solution)/shard_map/all_to_all | solution.py:44
  116.8 57.6 %all-to-all-start.1 = ((bf16[8,8,18,1024]{3,1,2,0:T(8,128)(2,1)}), bf16[8,8,18,1024]{3,1,2,0:T(8,128)(2,1)}, u32[]{:S(2)}, u32[]{:S(2)}) async-start(bf16[8,8,18,1024]{3,1,2,0:T(8,128)(2,1)} %stack.4), calls=%async_computation.1 | async-start | bytes 4718592 | tf_op jit(solution)/shard_map/all_to_all | solution.py:44
  121.2 156.4 %reduce-scatter.7.cloned.1.call-start = ((), (), s32[]{:S(2)}) async-start(), calls=%async_computation.11 | async-start | bytes 7077888 | tf_op jit(solution)/shard_map/reduce_scatter | solution.py:49
  183.6 4.4 copy-start.3
  190.0 1.0 copy-start.4
  200.3 156.9 %reduce-scatter.5.cloned.1.call-start = ((), (), s32[]{:S(2)}) async-start(), calls=%async_computation.10 | async-start | bytes 7077888 | tf_op jit(solution)/shard_map/reduce_scatter | solution.py:49
  211.1 186.8 %reduce-scatter.9.cloned.1.call-start = ((), (), s32[]{:S(2)}) async-start(), calls=%async_computation.12 | async-start | bytes 2359296 | tf_op jit(solution)/shard_map/reduce_scatter | solution.py:76
  216.3 222.5 %reduce-scatter.11.cloned.1.call-start = ((), (), s32[]{:S(2)}) async-start(), calls=%async_computation.13 | async-start | bytes 2359296 | tf_op jit(solution)/shard_map/reduce_scatter | solution.py:65
  220.5 145.9 %copy-start.2 = (s32[128]{0:T(128)S(1)}, s32[128]{0:T(128)}, u32[]{:S(2)}) copy-start(s32[128]{0:T(128)} %param.9) | copy-start | bytes 1540
  279.6 79.5 %all-to-all-start.5 = ((bf16[8,18,1024]{2,1,0:T(8,128)(2,1)}), bf16[8,18,1024]{2,1,0:T(8,128)(2,1)S(1)}, u32[]{:S(2)}, u32[]{:S(2)}) async-start(bf16[8,18,1024]{2,1,0:T(8,128)(2,1)} %convert_element_type.25), calls=%async_computation.7 | async-start | bytes 786432 | tf_op jit(solution)/shard_map/all_to_all | solution.py:51
  359.1 20.6 %all-to-all-start.2 = ((bf16[8,18,1024]{2,1,0:T(8,128)(2,1)}), bf16[8,18,1024]{2,1,0:T(8,128)(2,1)S(1)}, u32[]{:S(2)}, u32[]{:S(2)}) async-start(bf16[8,18,1024]{2,1,0:T(8,128)(2,1)} %convert_element_type.22), calls=%async_computation.3 | async-start | bytes 786432 | tf_op jit(solution)/shard_map/all_to_all | solution.py:51
Sparse Core Ops, SparseCore 0:
  200.5 77.1 reduce-scatter.6
  280.5 76.6 reduce-scatter.4
  360.6 37.1 reduce-scatter.8
  401.1 37.6 reduce-scatter.10
